TPU v7x, 32 devices: a whole 2x2x4 slice. The times are simulated.
32 devices in a mesh: row: 8 (over y, x, core), col: 4 (over z).
Axes of the slice: x: 2, y: 2, z: 4, core: 2. Of those that a mesh axis runs over, the one named last changes fastest.
Arguments:
- left_factors: float32 [128, 256, 32], P(None, ('row', 'col')), may hold values from -12 to 12
- right_factors: float32 [128, 128, 32], P(None, ('col', 'row')), may hold values from -12 to 12
- weight: float32 [1024, 128], replicated, may hold values from -0.1875 to 0.1875
- bias: float32 [128], replicated, may hold values from -2 to 2
- cotangent: float32 [256, 128, 128], P('row', 'col'), may hold values from -6 to 6
Outputs:
- pair_out: float32 [256, 128, 128], P('row', 'col')
- left_grad: float32 [128, 256, 32], P(None, ('row', 'col'))
- right_grad: float32 [128, 128, 32], P(None, ('col', 'row'))
- weight_grad: float32 [1024, 128], replicated
- bias_grad: float32 [128], replicated
All inputs are finite; a program needn't handle non-finite values.
Results may differ from a plain program's by a relative error of at most 0.0001.
Values sent between devices are 32-bit elements; how exact they have to be, the bound alone decides.
A program may use at most 64 MiB of HBM per device.

v0:
```python
import jax
import jax.numpy as jnp
from jax import lax
from jax.sharding import PartitionSpec as P


def per_device(left_factors, right_factors, weight, bias, cotangent):
    high = lax.Precision.HIGHEST
    samples = left_factors.shape[0]
    width = left_factors.shape[2]
    pair_width = weight.shape[1]
    left_all = lax.all_gather(left_factors, "col", axis=1, tiled=True)
    right_all = lax.all_gather(right_factors, "row", axis=1, tiled=True)
    tile_rows = left_all.shape[1]
    tile_cols = right_all.shape[1]
    step_rows = 16
    blocks = tile_rows // step_rows
    left_blocks = left_all.reshape(samples, blocks, step_rows, width).transpose(1, 0, 2, 3)
    cot_blocks = cotangent.reshape(blocks, step_rows, tile_cols, pair_width)

    def visit(carry, item):
        weight_sum, right_sum = carry
        left_block, cot_block = item
        outer = jnp.einsum("sic,sjd->ijcd", left_block, right_all, precision=high) / samples
        flat = outer.reshape(step_rows, tile_cols, width * width)
        pair_block = jnp.einsum("ijk,ke->ije", flat, weight, precision=high) + bias
        grad_flat = jnp.einsum("ije,ke->ijk", cot_block, weight, precision=high)
        weight_sum = weight_sum + jnp.einsum("ijk,ije->ke", flat, cot_block, precision=high)
        grad_outer = grad_flat.reshape(step_rows, tile_cols, width, width)
        left_block_grad = (
            jnp.einsum("ijcd,sjd->sic", grad_outer, right_all, precision=high) / samples
        )
        right_sum = (
            right_sum
            + jnp.einsum("ijcd,sic->sjd", grad_outer, left_block, precision=high) / samples
        )
        return ((weight_sum, right_sum), (pair_block, left_block_grad))

    start = (
        jnp.zeros((width * width, pair_width), jnp.float32),
        jnp.zeros((samples, tile_cols, width), jnp.float32),
    )
    (weight_part, right_part), (pair_blocks, left_pieces) = lax.scan(
        visit, start, (left_blocks, cot_blocks)
    )
    pair_out = pair_blocks.reshape(tile_rows, tile_cols, pair_width)
    left_part = left_pieces.transpose(1, 0, 2, 3).reshape(samples, tile_rows, width)
    bias_part = jnp.sum(cotangent, axis=(0, 1))
    left_total = lax.psum(left_part, "col")
    right_total = lax.psum(right_part, "row")
    left_share = tile_rows // lax.axis_size("col")
    right_share = tile_cols // lax.axis_size("row")
    left_grad = lax.dynamic_slice_in_dim(
        left_total, lax.axis_index("col") * left_share, left_share, 1
    )
    right_grad = lax.dynamic_slice_in_dim(
        right_total, lax.axis_index("row") * right_share, right_share, 1
    )
    weight_half, bias_half = lax.psum((weight_part, bias_part), "col")
    weight_total, bias_total = lax.psum((weight_half, bias_half), "row")
    total_rows = tile_rows * lax.axis_size("row")
    weight_grad = weight_total / total_rows
    bias_grad = bias_total / total_rows
    return (pair_out, left_grad, right_grad, weight_grad, bias_grad)


def solution(mesh):
    in_specs = (
        P(None, ("row", "col"), None),
        P(None, ("col", "row"), None),
        P(),
        P(),
        P("row", "col", None),
    )
    out_specs = (
        P("row", "col", None),
        P(None, ("row", "col"), None),
        P(None, ("col", "row"), None),
        P(),
        P(),
    )
    return jax.shard_map(
        per_device, mesh=mesh, in_specs=in_specs, out_specs=out_specs, check_vma=False
    )
```

profile of v0, /device:TPU:0, one launch (start us, length us, event | category | flops | bytes accessed | tf_op | source)
XLA Modules:
  0.0 329.0 jit_solution(1549016555022079670)
XLA Ops:
  7.2 11.6 %all_gather.7 = f32[128,32,32]{0,2,1:T(8,128)S(1)} all-gather(f32[128,4,32]{0,2,1:T(8,128)} %param.8), channel_id=1, replica_groups=mesh['row'=8,'col'=4] {'row'}, dimensions={1}, use_global_device_ids=true | all-gather | bytes 589824 | tf_op jit(solution)/shard_map/all_gather | solution.py:13
  19.2 16.6 %all_gather.6 = f32[128,32,32]{0,2,1:T(8,128)S(1)} all-gather(f32[128,8,32]{0,2,1:T(8,128)} %param.7), channel_id=1, replica_groups=mesh['row'=8,'col'=4] {'col'}, dimensions={1}, use_global_device_ids=true | all-gather | bytes 655360 | tf_op jit(solution)/shard_map/all_gather | solution.py:12
  35.7 170.8 %while.17 = (s32[]{:T(128)}, f32[1024,128]{1,0:T(8,128)}, f32[128,32,32]{0,2,1:T(8,128)}, f32[2,16,32,128]{3,2,1,0:T(8,128)}, f32[2,128,16,32]{1,3,2,0:T(8,128)}...) while((s32[]{:T(128)}, f32[1024,128]{1,0:T(8,128)}, ...), condition=%wide.region_1.2_spmd.clone, body=%wide.region_0.1_spmd.clone.sunk | while | flops 4833148928 | bytes 49812356 | solution.py:43
  59.1 0.8 copy-done.2
  59.9 9.1 %multiply_bitcast_fusion.2 = f32[16,32,32,32]{3,2,1,0:T(8,128)} fusion(f32[128,32,32]{0,1,2:T(8,128)S(1)} %get-tuple-element.222, f32[2,128,16,32]{1,3,2,0:T(8,128)S(1)} %get-tuple-element.221, s32[]{:T(128)} %get-tuple-element.204), kind=kOutput, calls=%fused_computation.2.clone.1 | convolution fusion | flops 805830656 | bytes 2883588 | tf_op jit(solution)/shard_map/while/body/eval_jaxpr/sic,sjd->ijcd/dot_general | solution.py:24
  68.9 6.7 %reshape.43 = f32[16,32,1024]{2,1,0:T(8,128)S(1)} reshape(f32[16,32,32,32]{3,2,1,0:T(8,128)} %multiply_bitcast_fusion.2) | data formatting | bytes 4194304 | tf_op jit(solution)/shard_map/while/body/eval_jaxpr/reshape | solution.py:25
  75.7 5.2 %fusion.67 = f32[1024,128]{1,0:T(8,128)} fusion(f32[16,32,1024]{2,1,0:T(8,128)S(1)} %reshape.43, f32[1024,128]{1,0:T(8,128)} %get-tuple-element.205, pred[]{:T(512)S(6)} %compare.3, f32[2,16,32,128]{3,2,1,0:T(8,128)} %get-tuple-element.223, s32[]{:T(128)} %get-tuple-element.204), kind=kOutput, calls=%fused_computation.5.clone.1 | convolution fusion | flops 805568512 | bytes 3408385 | tf_op jit(solution)/shard_map/while/body/eval_jaxpr/ijk,ije->ke/dot_general | solution.py:28
  80.9 7.7 %fusion.68 = f32[16,32,32,32]{3,1,2,0:T(8,128)S(1)} fusion(f32[32,32,128,1]{2,1,0,3:T(8,128)S(1)} %bitcast.110, f32[2,16,32,128]{3,2,1,0:T(8,128)} %get-tuple-element.223, s32[]{:T(128)} %get-tuple-element.204), kind=kOutput, calls=%fused_computation.19.clone.1 | convolution fusion | flops 805306368 | bytes 2884096 | tf_op jit(solution)/shard_map/while/body/eval_jaxpr/ije,ke->ijk/dot_general | solution.py:27
  88.6 3.2 copy-done
  91.8 17.0 %fusion.69 = f32[128,32,32]{0,2,1:T(8,128)S(1)} fusion(f32[16,32,32,32]{3,1,2,0:T(8,128)S(1)} %fusion.68, f32[128,32,32]{0,2,1:T(8,128)S(1)} %copy-done.4, pred[]{:T(512)S(6)} %compare.3, f32[2,128,16,32]{1,3,2,0:T(8,128)} %copy-done.2, s32[]{:T(128)} %get-tuple-element.204), kind=kOutput, calls=%fused_computation.7.clone.1 | convolution fusion | flops 805699584 | bytes 3408385 | tf_op jit(solution)/shard_map/while/body/eval_jaxpr/ijcd,sic->sjd/dot_general | solution.py:35
  109.6 2.5 fusion.70
  112.1 10.6 %copy.39 = f32[16,32,32,32]{1,2,3,0:T(8,128)} copy(f32[16,32,32,32]{3,1,2,0:T(8,128)} %copy-done) | data formatting | bytes 4194304 | tf_op jit(solution)/shard_map/while/body/eval_jaxpr/ije,ke->ijk/dot_general | solution.py:27
  122.7 9.2 %fusion.71 = f32[2,128,16,32]{1,3,2,0:T(8,128)S(1)} fusion(f32[2,128,16,32]{1,3,2,0:T(8,128)S(1)} %copy-done.6, s32[]{:T(128)} %get-tuple-element.204, f32[16,32,32,32]{1,2,3,0:T(8,128)} %copy.39, f32[128,32,32]{0,1,2:T(8,128)S(1)} %get-tuple-element.222), kind=kOutput, calls=%fused_computation.14.clone.1 | convolution fusion | flops 805371904 | bytes 2883588 | tf_op jit(solution)/shard_map/while/body/eval_jaxpr/ijcd,sjd->sic/dot_general | solution.py:31
  132.7 0.8 copy-done.2
  133.5 9.0 %multiply_bitcast_fusion.2 = f32[16,32,32,32]{3,2,1,0:T(8,128)} fusion(f32[128,32,32]{0,1,2:T(8,128)S(1)} %get-tuple-element.222, f32[2,128,16,32]{1,3,2,0:T(8,128)S(1)} %get-tuple-element.221, s32[]{:T(128)} %get-tuple-element.204), kind=kOutput, calls=%fused_computation.2.clone.1 | convolution fusion | flops 805830656 | bytes 2883588 | tf_op jit(solution)/shard_map/while/body/eval_jaxpr/sic,sjd->ijcd/dot_general | solution.py:24
  142.6 6.7 %reshape.43 = f32[16,32,1024]{2,1,0:T(8,128)S(1)} reshape(f32[16,32,32,32]{3,2,1,0:T(8,128)} %multiply_bitcast_fusion.2) | data formatting | bytes 4194304 | tf_op jit(solution)/shard_map/while/body/eval_jaxpr/reshape | solution.py:25
  149.3 5.4 %fusion.67 = f32[1024,128]{1,0:T(8,128)} fusion(f32[16,32,1024]{2,1,0:T(8,128)S(1)} %reshape.43, f32[1024,128]{1,0:T(8,128)} %get-tuple-element.205, pred[]{:T(512)S(6)} %compare.3, f32[2,16,32,128]{3,2,1,0:T(8,128)} %get-tuple-element.223, s32[]{:T(128)} %get-tuple-element.204), kind=kOutput, calls=%fused_computation.5.clone.1 | convolution fusion | flops 805568512 | bytes 3408385 | tf_op jit(solution)/shard_map/while/body/eval_jaxpr/ijk,ije->ke/dot_general | solution.py:28
  154.7 7.7 %fusion.68 = f32[16,32,32,32]{3,1,2,0:T(8,128)S(1)} fusion(f32[32,32,128,1]{2,1,0,3:T(8,128)S(1)} %bitcast.110, f32[2,16,32,128]{3,2,1,0:T(8,128)} %get-tuple-element.223, s32[]{:T(128)} %get-tuple-element.204), kind=kOutput, calls=%fused_computation.19.clone.1 | convolution fusion | flops 805306368 | bytes 2884096 | tf_op jit(solution)/shard_map/while/body/eval_jaxpr/ije,ke->ijk/dot_general | solution.py:27
  162.4 3.2 copy-done
  165.6 17.0 %fusion.69 = f32[128,32,32]{0,2,1:T(8,128)S(1)} fusion(f32[16,32,32,32]{3,1,2,0:T(8,128)S(1)} %fusion.68, f32[128,32,32]{0,2,1:T(8,128)S(1)} %copy-done.4, pred[]{:T(512)S(6)} %compare.3, f32[2,128,16,32]{1,3,2,0:T(8,128)} %copy-done.2, s32[]{:T(128)} %get-tuple-element.204), kind=kOutput, calls=%fused_computation.7.clone.1 | convolution fusion | flops 805699584 | bytes 3408385 | tf_op jit(solution)/shard_map/while/body/eval_jaxpr/ijcd,sic->sjd/dot_general | solution.py:35
  183.4 2.5 fusion.70
  185.9 10.6 %copy.39 = f32[16,32,32,32]{1,2,3,0:T(8,128)} copy(f32[16,32,32,32]{3,1,2,0:T(8,128)} %copy-done) | data formatting | bytes 4194304 | tf_op jit(solution)/shard_map/while/body/eval_jaxpr/ije,ke->ijk/dot_general | solution.py:27
  196.5 9.2 %fusion.71 = f32[2,128,16,32]{1,3,2,0:T(8,128)S(1)} fusion(f32[2,128,16,32]{1,3,2,0:T(8,128)S(1)} %copy-done.6, s32[]{:T(128)} %get-tuple-element.204, f32[16,32,32,32]{1,2,3,0:T(8,128)} %copy.39, f32[128,32,32]{0,1,2:T(8,128)S(1)} %get-tuple-element.222), kind=kOutput, calls=%fused_computation.14.clone.1 | convolution fusion | flops 805371904 | bytes 2883588 | tf_op jit(solution)/shard_map/while/body/eval_jaxpr/ijcd,sjd->sic/dot_general | solution.py:31
  205.7 0.8 copy-done.7
  206.6 52.6 %all-reduce.7.cloned.1.call-done = (f32[128,32,32]{0,2,1:T(8,128)}, f32[1024,128]{1,0:T(8,128)}) async-done(((f32[128,32,32]{0,2,1:T(8,128)}, f32[1024,128]{1,0:T(8,128)}), (f32[128,32,32]{0,2,1:T(8,128)}, f32[1024,128]{1,0:T(8,128)})) %all-reduce.7.cloned.1.call-update) | async-done | bytes 1048592 | tf_op jit(solution)/shard_map/psum | solution.py:49
  259.2 1.2 reduce_sum.9
  260.4 10.0 %psum.46 = f32[128]{0:T(128)S(1)} all-reduce(f32[128]{0:T(128)S(1)} %reduce_sum.9), channel_id=1, replica_groups=mesh['row'=8,'col'=4] {'col'}, use_global_device_ids=true, to_apply=%region_7.8 | all-reduce | flops 128 | bytes 1024 | tf_op jit(solution)/shard_map/psum | solution.py:59
  270.4 11.8 %psum.47 = f32[128]{0:T(128)S(1)} all-reduce(f32[128]{0:T(128)S(1)} %psum.46), channel_id=1, replica_groups=mesh['row'=8,'col'=4] {'row'}, use_global_device_ids=true, to_apply=%region_8.9 | all-reduce | flops 128 | bytes 1024 | tf_op jit(solution)/shard_map/psum | solution.py:60
  282.8 1.6 constant_dynamic-slice_fusion.1
  284.4 34.1 %all-reduce.5.cloned.1.call-done = (f32[128,32,32]{0,2,1:T(8,128)}, f32[1024,128]{1,0:T(8,128)}) async-done(((f32[128,32,32]{0,2,1:T(8,128)}, f32[1024,128]{1,0:T(8,128)}), (f32[128,32,32]{0,2,1:T(8,128)}, f32[1024,128]{1,0:T(8,128)})) %all-reduce.5.cloned.1.call-update) | async-done | bytes 1048592 | tf_op jit(solution)/shard_map/psum | solution.py:50
  318.5 1.9 broadcast_multiply_fusion
  320.3 1.5 constant_dynamic-slice_fusion
  (41 shorter events, 3.3 us)
Async XLA Ops:
  7.2 252.0 %all-reduce.7.cloned.1.call-start = ((), (), s32[]{:S(2)}) async-start(), calls=%async_computation.1 | async-start | bytes 2097152 | tf_op jit(solution)/shard_map/psum | solution.py:49
  59.1 0.8 copy-start.2
  68.9 12.0 %copy-start.1 = (f32[1024,128]{1,0:T(8,128)S(1)}, f32[1024,128]{1,0:T(8,128)}, u32[]{:S(2)}) copy-start(f32[1024,128]{1,0:T(8,128)} %get-tuple-element.224) | copy-start | bytes 1572868 | tf_op jit(solution)/shard_map/while
  75.6 16.1 %copy-start.4 = (f32[128,32,32]{0,2,1:T(8,128)S(1)}, f32[128,32,32]{0,2,1:T(8,128)}, u32[]{:S(2)}) copy-start(f32[128,32,32]{0,2,1:T(8,128)} %get-tuple-element.206) | copy-start | bytes 1572868 | tf_op jit(solution)/shard_map/while
  80.9 28.7 %copy-start.8 = (f32[128]{0:T(128)S(1)}, f32[128]{0:T(128)}, u32[]{:S(2)}) copy-start(f32[128]{0:T(128)} %get-tuple-element.225) | copy-start | bytes 1540 | tf_op jit(solution)/shard_map/while
  88.6 3.2 copy-start
  108.8 0.8 copy-start.5
  112.1 10.6 %copy-start.6 = (f32[2,128,16,32]{1,3,2,0:T(8,128)S(1)}, f32[2,128,16,32]{1,3,2,0:T(8,128)}, u32[]{:S(2)}) copy-start(f32[2,128,16,32]{1,3,2,0:T(8,128)} %get-tuple-element.208) | copy-start | bytes 1572868 | tf_op jit(solution)/shard_map/while
  122.7 10.0 %copy-start.3 = (f32[2,128,16,32]{1,3,2,0:T(8,128)S(1)}, f32[2,128,16,32]{1,3,2,0:T(8,128)}, u32[]{:S(2)}) copy-start(f32[2,128,16,32]{1,3,2,0:T(8,128)} %copy-done.2) | copy-start | bytes 1572868 | tf_op jit(solution)/shard_map/while
  131.9 0.8 copy-start.7
  132.7 0.8 copy-start.2
  142.6 12.1 %copy-start.1 = (f32[1024,128]{1,0:T(8,128)S(1)}, f32[1024,128]{1,0:T(8,128)}, u32[]{:S(2)}) copy-start(f32[1024,128]{1,0:T(8,128)} %get-tuple-element.224) | copy-start | bytes 1572868 | tf_op jit(solution)/shard_map/while
  149.3 16.3 %copy-start.4 = (f32[128,32,32]{0,2,1:T(8,128)S(1)}, f32[128,32,32]{0,2,1:T(8,128)}, u32[]{:S(2)}) copy-start(f32[128,32,32]{0,2,1:T(8,128)} %get-tuple-element.206) | copy-start | bytes 1572868 | tf_op jit(solution)/shard_map/while
  154.7 28.7 %copy-start.8 = (f32[128]{0:T(128)S(1)}, f32[128]{0:T(128)}, u32[]{:S(2)}) copy-start(f32[128]{0:T(128)} %get-tuple-element.225) | copy-start | bytes 1540 | tf_op jit(solution)/shard_map/while
  162.4 3.2 copy-start
  182.6 0.8 copy-start.5
  185.9 10.6 %copy-start.6 = (f32[2,128,16,32]{1,3,2,0:T(8,128)S(1)}, f32[2,128,16,32]{1,3,2,0:T(8,128)}, u32[]{:S(2)}) copy-start(f32[2,128,16,32]{1,3,2,0:T(8,128)} %get-tuple-element.208) | copy-start | bytes 1572868 | tf_op jit(solution)/shard_map/while
  196.5 10.0 %copy-start.3 = (f32[2,128,16,32]{1,3,2,0:T(8,128)S(1)}, f32[2,128,16,32]{1,3,2,0:T(8,128)}, u32[]{:S(2)}) copy-start(f32[2,128,16,32]{1,3,2,0:T(8,128)} %copy-done.2) | copy-start | bytes 1572868 | tf_op jit(solution)/shard_map/while
  205.7 0.8 copy-start.7
  206.6 111.9 %all-reduce.5.cloned.1.call-start = ((), (), s32[]{:S(2)}) async-start(), calls=%async_computation | async-start | bytes 2097152 | tf_op jit(solution)/shard_map/psum | solution.py:50
Sparse Core Ops, SparseCore 0:
  206.7 52.4 all-reduce.6
  262.4 56.0 all-reduce.4
where the time goes:
time: 332 us; the launch traced here: 329 us
  matrix products  101 us (30%)
  waiting for transfers between devices  86.7 us (26%)
  blocking collectives  50 us (15%)
  local copies, waits for them, and re-layouts  49.2 us (15%)
  loops' own time  23.5 us (7%)
  between operations  14.5 us (4%)
  other arithmetic  3.58 us (1%)
    psum x1, waiting for transfers between devices, per_device(): left_total = lax.psum(left_part, 'col')  52.6 us
    psum x1, waiting for transfers between devices, per_device(): right_total = lax.psum(right_part, 'row')  34.1 us
    dot_general x2, matrix products, visit(): jnp.einsum('ijcd,sic->sjd', grad_outer, left_block, precision=high)  33.9 us
    another operation x1, loops' own time, per_device(): lax.scan(visit, start, (left_blocks, cot_blocks))  23.5 us
    dot_general x2, local copies, waits for them, and re-layouts, visit(): grad_flat = jnp.einsum('ije,ke->ijk', cot_block, weight, precision=high)  21.3 us
    dot_general x2, matrix products, visit(): jnp.einsum('ijcd,sjd->sic', grad_outer, right_all, precision=high) / samples  18.4 us
    dot_general x2, matrix products, visit(): jnp.einsum('sic,sjd->ijcd', left_block, right_all, precision=high) / samples  18.1 us
    all_gather x1, blocking collectives, per_device(): left_all = lax.all_gather(left_factors, 'col', axis=1, tiled=True)  16.6 us
  transfers between devices with their start and end apart: 2, of which 2 were waited for; matrix products, arithmetic and copies ran while one was open for 1% of the time, Pallas kernels for 0%

commit v1 on v0

--- a/solution.py
+++ b/solution.py
@@ -46,7 +46,20 @@
     pair_out = pair_blocks.reshape(tile_rows, tile_cols, pair_width)
     left_part = left_pieces.transpose(1, 0, 2, 3).reshape(samples, tile_rows, width)
     bias_part = jnp.sum(cotangent, axis=(0, 1))
-    left_total = lax.psum(left_part, "col")
+
+    def change_sums_all(local_array, axis_key):
+        n_axis = lax.psum(1, axis_name=axis_key)
+        state_now = local_array
+        for p in [
+            [(rr, rr ^ dev_i) for rr in range(n_axis)]
+            for dev_i in (1, 2, 4, 8, 16)
+            if dev_i < n_axis
+        ]:
+            answer = lax.ppermute(state_now, perm=p, axis_name=axis_key)
+            state_now = state_now + answer
+        return state_now
+
+    left_total = change_sums_all(left_part, "col")
     right_total = lax.psum(right_part, "row")
     left_share = tile_rows // lax.axis_size("col")
     right_share = tile_cols // lax.axis_size("row")

time: 332 us -> 321 us (0.967)
  waiting for transfers between devices: 86.7 us -> 73.5 us
    psum x1, waiting for transfers between devices: 52.6 us -> 39.1 us  [per_device(): weight_half, bias_half = lax.psum((weight_part, bias_part), 'col')]
  transfers between devices with their start and end apart: 2 -> 4, of which waited for: 2 -> 2; matrix products, arithmetic and copies ran while one was open for 1% -> 2% of each run, Pallas kernels for 0% -> 0%
where the time goes in v1:
time: 321 us; the launch traced here: 319 us
  matrix products  101 us (31%)
  waiting for transfers between devices  73.5 us (23%)
  blocking collectives  50.6 us (16%)
  local copies, waits for them, and re-layouts  47.6 us (15%)
  loops' own time  23.7 us (7%)
  between operations  14.5 us (5%)
  other arithmetic  5.38 us (2%)
    psum x1, waiting for transfers between devices, per_device(): weight_half, bias_half = lax.psum((weight_part, bias_part), 'col')  39.1 us
    psum x1, waiting for transfers between devices, per_device(): right_total = lax.psum(right_part, 'row')  34.4 us
    dot_general x2, matrix products, visit(): jnp.einsum('ijcd,sic->sjd', grad_outer, left_block, precision=high)  33.9 us
    another operation x1, loops' own time, per_device(): lax.scan(visit, start, (left_blocks, cot_blocks))  23.7 us
    dot_general x2, local copies, waits for them, and re-layouts, visit(): grad_flat = jnp.einsum('ije,ke->ijk', cot_block, weight, precision=high)  21.3 us
    dot_general x2, matrix products, visit(): jnp.einsum('ijcd,sjd->sic', grad_outer, right_all, precision=high) / samples  18.4 us
    dot_general x2, matrix products, visit(): jnp.einsum('sic,sjd->ijcd', left_block, right_all, precision=high) / samples  18.1 us
    all_gather x1, blocking collectives, per_device(): left_all = lax.all_gather(left_factors, 'col', axis=1, tiled=True)  16.6 us
  transfers between devices with their start and end apart: 4, of which 2 were waited for; matrix products, arithmetic and copies ran while one was open for 2% of the time, Pallas kernels for 0%

profile of v1, /device:TPU:0, one launch (start us, length us, event | category | flops | bytes accessed | tf_op | source)
XLA Modules:
  0.0 318.9 jit_solution(16383405498086125573)
XLA Ops:
  7.2 11.6 %all_gather.7 = f32[128,32,32]{0,2,1:T(8,128)S(1)} all-gather(f32[128,4,32]{0,2,1:T(8,128)} %param.8), channel_id=1, replica_groups=mesh['row'=8,'col'=4] {'row'}, dimensions={1}, use_global_device_ids=true | all-gather | bytes 589824 | tf_op jit(solution)/shard_map/all_gather | solution.py:13
  19.2 16.6 %all_gather.6 = f32[128,32,32]{0,2,1:T(8,128)S(1)} all-gather(f32[128,8,32]{0,2,1:T(8,128)} %param.7), channel_id=1, replica_groups=mesh['row'=8,'col'=4] {'col'}, dimensions={1}, use_global_device_ids=true | all-gather | bytes 655360 | tf_op jit(solution)/shard_map/all_gather | solution.py:12
  35.7 171.0 %while.17 = (s32[]{:T(128)}, f32[1024,128]{1,0:T(8,128)}, f32[128,32,32]{0,2,1:T(8,128)}, f32[2,16,32,128]{3,2,1,0:T(8,128)}, f32[2,128,16,32]{1,3,2,0:T(8,128)}...) while((s32[]{:T(128)}, f32[1024,128]{1,0:T(8,128)}, ...), condition=%wide.region_1.2_spmd.clone, body=%wide.region_0.1_spmd.clone.sunk | while | flops 4833148928 | bytes 49812356 | solution.py:43
  60.0 9.0 %multiply_bitcast_fusion.2 = f32[16,32,32,32]{3,2,1,0:T(8,128)} fusion(f32[128,32,32]{0,1,2:T(8,128)S(1)} %get-tuple-element.220, f32[2,128,16,32]{1,3,2,0:T(8,128)S(1)} %get-tuple-element.219, s32[]{:T(128)} %get-tuple-element.202), kind=kOutput, calls=%fused_computation.2.clone.1 | convolution fusion | flops 805830656 | bytes 2883588 | tf_op jit(solution)/shard_map/while/body/eval_jaxpr/sic,sjd->ijcd/dot_general | solution.py:24
  69.1 6.7 %reshape.43 = f32[16,32,1024]{2,1,0:T(8,128)S(1)} reshape(f32[16,32,32,32]{3,2,1,0:T(8,128)} %multiply_bitcast_fusion.2) | data formatting | bytes 4194304 | tf_op jit(solution)/shard_map/while/body/eval_jaxpr/reshape | solution.py:25
  75.8 5.2 %fusion.67 = f32[1024,128]{1,0:T(8,128)} fusion(f32[16,32,1024]{2,1,0:T(8,128)S(1)} %reshape.43, f32[1024,128]{1,0:T(8,128)} %get-tuple-element.203, pred[]{:T(512)S(6)} %compare.3, f32[2,16,32,128]{3,2,1,0:T(8,128)} %get-tuple-element.221, s32[]{:T(128)} %get-tuple-element.202), kind=kOutput, calls=%fused_computation.5.clone.1 | convolution fusion | flops 805568512 | bytes 3408385 | tf_op jit(solution)/shard_map/while/body/eval_jaxpr/ijk,ije->ke/dot_general | solution.py:28
  81.1 7.7 %fusion.68 = f32[16,32,32,32]{3,1,2,0:T(8,128)S(1)} fusion(f32[32,32,128,1]{2,1,0,3:T(8,128)S(1)} %bitcast.111, f32[2,16,32,128]{3,2,1,0:T(8,128)} %get-tuple-element.221, s32[]{:T(128)} %get-tuple-element.202), kind=kOutput, calls=%fused_computation.19.clone.1 | convolution fusion | flops 805306368 | bytes 2884096 | tf_op jit(solution)/shard_map/while/body/eval_jaxpr/ije,ke->ijk/dot_general | solution.py:27
  88.7 3.2 %copy-done = f32[16,32,32,32]{3,1,2,0:T(8,128)} copy-done((f32[16,32,32,32]{3,1,2,0:T(8,128)}, f32[16,32,32,32]{3,1,2,0:T(8,128)S(1)}, u32[]{:S(2)}) %copy-start) | copy-done | bytes 2097176 | tf_op jit(solution)/shard_map/while
  91.9 17.0 %fusion.69 = f32[128,32,32]{0,2,1:T(8,128)S(1)} fusion(f32[16,32,32,32]{3,1,2,0:T(8,128)S(1)} %fusion.68, f32[128,32,32]{0,2,1:T(8,128)S(1)} %copy-done.4, pred[]{:T(512)S(6)} %compare.3, f32[2,128,16,32]{1,3,2,0:T(8,128)} %copy-done.2, s32[]{:T(128)} %get-tuple-element.202), kind=kOutput, calls=%fused_computation.7.clone.1 | convolution fusion | flops 805699584 | bytes 3408385 | tf_op jit(solution)/shard_map/while/body/eval_jaxpr/ijcd,sic->sjd/dot_general | solution.py:35
  109.7 2.5 fusion.70
  112.2 10.6 %copy.39 = f32[16,32,32,32]{1,2,3,0:T(8,128)} copy(f32[16,32,32,32]{3,1,2,0:T(8,128)} %copy-done) | data formatting | bytes 4194304 | tf_op jit(solution)/shard_map/while/body/eval_jaxpr/ije,ke->ijk/dot_general | solution.py:27
  122.9 9.2 %fusion.71 = f32[2,128,16,32]{1,3,2,0:T(8,128)S(1)} fusion(f32[2,128,16,32]{1,3,2,0:T(8,128)S(1)} %copy-done.6, s32[]{:T(128)} %get-tuple-element.202, f32[16,32,32,32]{1,2,3,0:T(8,128)} %copy.39, f32[128,32,32]{0,1,2:T(8,128)S(1)} %get-tuple-element.220), kind=kOutput, calls=%fused_computation.14.clone.1 | convolution fusion | flops 805371904 | bytes 2883588 | tf_op jit(solution)/shard_map/while/body/eval_jaxpr/ijcd,sjd->sic/dot_general | solution.py:31
  132.9 0.8 copy-done.2
  133.7 9.0 %multiply_bitcast_fusion.2 = f32[16,32,32,32]{3,2,1,0:T(8,128)} fusion(f32[128,32,32]{0,1,2:T(8,128)S(1)} %get-tuple-element.220, f32[2,128,16,32]{1,3,2,0:T(8,128)S(1)} %get-tuple-element.219, s32[]{:T(128)} %get-tuple-element.202), kind=kOutput, calls=%fused_computation.2.clone.1 | convolution fusion | flops 805830656 | bytes 2883588 | tf_op jit(solution)/shard_map/while/body/eval_jaxpr/sic,sjd->ijcd/dot_general | solution.py:24
  142.7 6.7 %reshape.43 = f32[16,32,1024]{2,1,0:T(8,128)S(1)} reshape(f32[16,32,32,32]{3,2,1,0:T(8,128)} %multiply_bitcast_fusion.2) | data formatting | bytes 4194304 | tf_op jit(solution)/shard_map/while/body/eval_jaxpr/reshape | solution.py:25
  149.5 5.4 %fusion.67 = f32[1024,128]{1,0:T(8,128)} fusion(f32[16,32,1024]{2,1,0:T(8,128)S(1)} %reshape.43, f32[1024,128]{1,0:T(8,128)} %get-tuple-element.203, pred[]{:T(512)S(6)} %compare.3, f32[2,16,32,128]{3,2,1,0:T(8,128)} %get-tuple-element.221, s32[]{:T(128)} %get-tuple-element.202), kind=kOutput, calls=%fused_computation.5.clone.1 | convolution fusion | flops 805568512 | bytes 3408385 | tf_op jit(solution)/shard_map/while/body/eval_jaxpr/ijk,ije->ke/dot_general | solution.py:28
  154.9 7.7 %fusion.68 = f32[16,32,32,32]{3,1,2,0:T(8,128)S(1)} fusion(f32[32,32,128,1]{2,1,0,3:T(8,128)S(1)} %bitcast.111, f32[2,16,32,128]{3,2,1,0:T(8,128)} %get-tuple-element.221, s32[]{:T(128)} %get-tuple-element.202), kind=kOutput, calls=%fused_computation.19.clone.1 | convolution fusion | flops 805306368 | bytes 2884096 | tf_op jit(solution)/shard_map/while/body/eval_jaxpr/ije,ke->ijk/dot_general | solution.py:27
  162.5 3.2 %copy-done = f32[16,32,32,32]{3,1,2,0:T(8,128)} copy-done((f32[16,32,32,32]{3,1,2,0:T(8,128)}, f32[16,32,32,32]{3,1,2,0:T(8,128)S(1)}, u32[]{:S(2)}) %copy-start) | copy-done | bytes 2097176 | tf_op jit(solution)/shard_map/while
  165.8 17.0 %fusion.69 = f32[128,32,32]{0,2,1:T(8,128)S(1)} fusion(f32[16,32,32,32]{3,1,2,0:T(8,128)S(1)} %fusion.68, f32[128,32,32]{0,2,1:T(8,128)S(1)} %copy-done.4, pred[]{:T(512)S(6)} %compare.3, f32[2,128,16,32]{1,3,2,0:T(8,128)} %copy-done.2, s32[]{:T(128)} %get-tuple-element.202), kind=kOutput, calls=%fused_computation.7.clone.1 | convolution fusion | flops 805699584 | bytes 3408385 | tf_op jit(solution)/shard_map/while/body/eval_jaxpr/ijcd,sic->sjd/dot_general | solution.py:35
  183.5 2.5 fusion.70
  186.0 10.6 %copy.39 = f32[16,32,32,32]{1,2,3,0:T(8,128)} copy(f32[16,32,32,32]{3,1,2,0:T(8,128)} %copy-done) | data formatting | bytes 4194304 | tf_op jit(solution)/shard_map/while/body/eval_jaxpr/ije,ke->ijk/dot_general | solution.py:27
  196.7 9.2 %fusion.71 = f32[2,128,16,32]{1,3,2,0:T(8,128)S(1)} fusion(f32[2,128,16,32]{1,3,2,0:T(8,128)S(1)} %copy-done.6, s32[]{:T(128)} %get-tuple-element.202, f32[16,32,32,32]{1,2,3,0:T(8,128)} %copy.39, f32[128,32,32]{0,1,2:T(8,128)S(1)} %get-tuple-element.220), kind=kOutput, calls=%fused_computation.14.clone.1 | convolution fusion | flops 805371904 | bytes 2883588 | tf_op jit(solution)/shard_map/while/body/eval_jaxpr/ijcd,sjd->sic/dot_general | solution.py:31
  205.9 0.8 copy-done.7
  206.8 1.9 collective-permute-start
  208.7 39.1 %all-reduce.4.cloned.1.call-done = f32[1024,128]{1,0:T(8,128)} async-done(((f32[1024,128]{1,0:T(8,128)}), f32[1024,128]{1,0:T(8,128)}) %all-reduce.4.cloned.1.call-update) | async-done | bytes 524304 | tf_op jit(solution)/shard_map/psum | solution.py:72
  247.8 1.2 reduce_sum.9
  249.0 10.6 %psum.38 = f32[128]{0:T(128)S(1)} all-reduce(f32[128]{0:T(128)S(1)} %reduce_sum.9), channel_id=1, replica_groups=mesh['row'=8,'col'=4] {'col'}, use_global_device_ids=true, to_apply=%region_6.7 | all-reduce | flops 128 | bytes 1024 | tf_op jit(solution)/shard_map/psum | solution.py:72
  259.6 11.9 %psum.39 = f32[128]{0:T(128)S(1)} all-reduce(f32[128]{0:T(128)S(1)} %psum.38), channel_id=1, replica_groups=mesh['row'=8,'col'=4] {'row'}, use_global_device_ids=true, to_apply=%region_7.8 | all-reduce | flops 128 | bytes 1024 | tf_op jit(solution)/shard_map/psum | solution.py:73
  271.5 1.1 bitcast_add_fusion
  273.2 34.4 %all-reduce.6.cloned.1.call-done = (f32[128,32,32]{0,2,1:T(8,128)}, f32[1024,128]{1,0:T(8,128)}) async-done(((f32[128,32,32]{0,2,1:T(8,128)}, f32[1024,128]{1,0:T(8,128)}), (f32[128,32,32]{0,2,1:T(8,128)}, f32[1024,128]{1,0:T(8,128)})) %all-reduce.6.cloned.1.call-update) | async-done | bytes 1048592 | tf_op jit(solution)/shard_map/psum | solution.py:63
  307.6 1.5 constant_dynamic-slice_fusion
  309.1 1.9 broadcast_multiply_fusion
  (46 shorter events, 4.9 us)
Async XLA Ops:
  7.2 240.6 %all-reduce.4.cloned.1.call-start = ((), (), s32[]{:S(2)}) async-start(), calls=%async_computation | async-start | bytes 1048576 | tf_op jit(solution)/shard_map/psum | solution.py:72
  59.2 0.8 copy-start.2
  69.1 12.0 %copy-start.1 = (f32[1024,128]{1,0:T(8,128)S(1)}, f32[1024,128]{1,0:T(8,128)}, u32[]{:S(2)}) copy-start(f32[1024,128]{1,0:T(8,128)} %get-tuple-element.222) | copy-start | bytes 1572868 | tf_op jit(solution)/shard_map/while
  75.8 16.1 %copy-start.4 = (f32[128,32,32]{0,2,1:T(8,128)S(1)}, f32[128,32,32]{0,2,1:T(8,128)}, u32[]{:S(2)}) copy-start(f32[128,32,32]{0,2,1:T(8,128)} %get-tuple-element.204) | copy-start | bytes 1572868 | tf_op jit(solution)/shard_map/while
  81.1 28.7 %copy-start.8 = (f32[128]{0:T(128)S(1)}, f32[128]{0:T(128)}, u32[]{:S(2)}) copy-start(f32[128]{0:T(128)} %get-tuple-element.223) | copy-start | bytes 1540 | tf_op jit(solution)/shard_map/while
  88.7 3.2 %copy-start = (f32[16,32,32,32]{3,1,2,0:T(8,128)}, f32[16,32,32,32]{3,1,2,0:T(8,128)S(1)}, u32[]{:S(2)}) copy-start(f32[16,32,32,32]{3,1,2,0:T(8,128)S(1)} %fusion.68) | copy-start | bytes 6291460 | tf_op jit(solution)/shard_map/while
  108.9 0.8 copy-start.5
  112.2 10.6 %copy-start.6 = (f32[2,128,16,32]{1,3,2,0:T(8,128)S(1)}, f32[2,128,16,32]{1,3,2,0:T(8,128)}, u32[]{:S(2)}) copy-start(f32[2,128,16,32]{1,3,2,0:T(8,128)} %get-tuple-element.206) | copy-start | bytes 1572868 | tf_op jit(solution)/shard_map/while
  122.9 10.0 %copy-start.3 = (f32[2,128,16,32]{1,3,2,0:T(8,128)S(1)}, f32[2,128,16,32]{1,3,2,0:T(8,128)}, u32[]{:S(2)}) copy-start(f32[2,128,16,32]{1,3,2,0:T(8,128)} %copy-done.2) | copy-start | bytes 1572868 | tf_op jit(solution)/shard_map/while
  132.1 0.8 copy-start.7
  132.9 0.8 copy-start.2
  142.7 12.1 %copy-start.1 = (f32[1024,128]{1,0:T(8,128)S(1)}, f32[1024,128]{1,0:T(8,128)}, u32[]{:S(2)}) copy-start(f32[1024,128]{1,0:T(8,128)} %get-tuple-element.222) | copy-start | bytes 1572868 | tf_op jit(solution)/shard_map/while
  149.4 16.3 %copy-start.4 = (f32[128,32,32]{0,2,1:T(8,128)S(1)}, f32[128,32,32]{0,2,1:T(8,128)}, u32[]{:S(2)}) copy-start(f32[128,32,32]{0,2,1:T(8,128)} %get-tuple-element.204) | copy-start | bytes 1572868 | tf_op jit(solution)/shard_map/while
  154.9 28.7 %copy-start.8 = (f32[128]{0:T(128)S(1)}, f32[128]{0:T(128)}, u32[]{:S(2)}) copy-start(f32[128]{0:T(128)} %get-tuple-element.223) | copy-start | bytes 1540 | tf_op jit(solution)/shard_map/while
  162.5 3.2 %copy-start = (f32[16,32,32,32]{3,1,2,0:T(8,128)}, f32[16,32,32,32]{3,1,2,0:T(8,128)S(1)}, u32[]{:S(2)}) copy-start(f32[16,32,32,32]{3,1,2,0:T(8,128)S(1)} %fusion.68) | copy-start | bytes 6291460 | tf_op jit(solution)/shard_map/while
  182.7 0.8 copy-start.5
  186.0 10.6 %copy-start.6 = (f32[2,128,16,32]{1,3,2,0:T(8,128)S(1)}, f32[2,128,16,32]{1,3,2,0:T(8,128)}, u32[]{:S(2)}) copy-start(f32[2,128,16,32]{1,3,2,0:T(8,128)} %get-tuple-element.206) | copy-start | bytes 1572868 | tf_op jit(solution)/shard_map/while
  196.7 10.0 %copy-start.3 = (f32[2,128,16,32]{1,3,2,0:T(8,128)S(1)}, f32[2,128,16,32]{1,3,2,0:T(8,128)}, u32[]{:S(2)}) copy-start(f32[2,128,16,32]{1,3,2,0:T(8,128)} %copy-done.2) | copy-start | bytes 1572868 | tf_op jit(solution)/shard_map/while
  205.9 0.8 copy-start.7
  206.7 100.9 %all-reduce.6.cloned.1.call-start = ((), (), s32[]{:S(2)}) async-start(), calls=%async_computation.1 | async-start | bytes 2097152 | tf_op jit(solution)/shard_map/psum | solution.py:63
  206.8 64.7 %collective-permute-start = (f32[128,32,32]{0,2,1:T(8,128)}, f32[128,32,32]{0,2,1:T(8,128)S(1)}, u32[]{:S(2)}, u32[]{:S(2)}) collective-permute-start(f32[128,32,32]{0,2,1:T(8,128)} %bitcast.115), channel_id=1, source_target_pairs={{0,1},{1,0},{2,3},{3,2},{4,5},{5,4},{6,7},{7,6},{8,9},{9,8},{10,11... | collective-permute-start | bytes 1572872 | tf_op jit(solution)/shard_map/ppermute | solution.py:58
  272.6 38.4 %collective-permute-start.1 = (f32[128,32,32]{0,2,1:T(8,128)S(1)}, f32[128,32,32]{0,2,1:T(8,128)S(1)}, u32[]{:S(2)}, u32[]{:S(2)}) collective-permute-start(f32[128,32,32]{0,2,1:T(8,128)S(1)} %bitcast_add_fusion), channel_id=1, source_target_pairs={{0,2},{1,3},{2,0},{3,1},{4,6},{5,7},{6,4},{7,5},{8,10},{9,11},{10,... | collective-permute-start | bytes 1572872 | tf_op jit(solution)/shard_map/ppermute | solution.py:58
Sparse Core Ops, SparseCore 0:
  206.8 40.8 all-reduce.3
  251.0 56.5 all-reduce.5
